TPU v7x, 32 devices: a whole 2x2x4 slice. The times are simulated.
32 devices in a mesh: dp: 8 (over z, y), tensor: 4 (over x, core).
Axes of the slice: x: 2, y: 2, z: 4, core: 2. Of those that a mesh axis runs over, the one named last changes fastest.
Arguments:
- hidden: bfloat16 [16384, 768], P('dp'), may hold values from -6 to 6
- cotangent: bfloat16 [16384, 768], P('dp'), may hold values from -6 to 6
- seg_ids: int32 [16384], P('dp'), may hold values from 0 to 1024, as said below
- counts: int32 [8], P('dp'), may hold values from 1024 to 2048, as said below
- norm_gain: float32 [768], replicated, may hold values from 0.5 to 1.5
- w_x: bfloat16 [768, 1536], P(None, 'tensor'), may hold values from -0.21875 to 0.21875
- w_z: bfloat16 [768, 1536], P(None, 'tensor'), may hold values from -0.21875 to 0.21875
- w_dt: bfloat16 [768, 24], P(None, 'tensor'), may hold values from -0.21875 to 0.21875
- w_bc: bfloat16 [768, 256], replicated, may hold values from -0.21875 to 0.21875
- conv_x: float32 [4, 1536], P(None, 'tensor'), may hold values from -3 to 3
- conv_x_bias: float32 [1536], P('tensor'), may hold values from -0.5 to 0.5
- conv_bc: float32 [4, 256], replicated, may hold values from -3 to 3
- conv_bc_bias: float32 [256], replicated, may hold values from -0.5 to 0.5
- dt_bias: float32 [24], P('tensor'), may hold values from -4 to -1
- a_log: float32 [24], P('tensor'), may hold values from -1 to 2.5
- d_skip: float32 [24], P('tensor'), may hold values from 0.5 to 1.5
- gate_gain: float32 [1536], P('tensor'), may hold values from 0.5 to 1.5
- w_out: bfloat16 [1536, 768], P('tensor'), may hold values from -0.15625 to 0.15625
Outputs:
- block_out: bfloat16 [16384, 768], P('dp')
- grad_hidden: float32 [16384, 768], P('dp')
- grad_norm_gain: float32 [768], replicated
- grad_w_x: float32 [768, 1536], P(None, 'tensor')
- grad_w_z: float32 [768, 1536], P(None, 'tensor')
- grad_w_dt: float32 [768, 24], P(None, 'tensor')
- grad_w_bc: float32 [768, 256], replicated
- grad_conv_x: float32 [4, 1536], P(None, 'tensor')
- grad_conv_x_bias: float32 [1536], P('tensor')
- grad_conv_bc: float32 [4, 256], replicated
- grad_conv_bc_bias: float32 [256], replicated
- grad_dt_bias: float32 [24], P('tensor')
- grad_a_log: float32 [24], P('tensor')
- grad_d_skip: float32 [24], P('tensor')
- grad_gate_gain: float32 [1536], P('tensor')
- grad_w_out: float32 [1536, 768], P('tensor')
Inputs may be any that keep to these rules, and one draw needn't show every extreme that they name: `seg_ids`: within each shard of 2048 slots the ids start at 0, never fall and rise by at most 1 from slot to slot; slots 0 to 1023 have id 0 and slot 1024 starts a new id; in some shard every slot from 1024 on starts a new id. `counts`: each shard's count is at least 1024; some shard is full in every draw.
All inputs are finite; a program needn't handle non-finite values.
Results may differ from a plain program's by a relative error of at most 0.012.
Values sent between devices are 32-bit elements; how exact they have to be, the bound alone decides.
No kernel may reach another device: no remote copies, remote signals or barrier semaphores. Data moves between devices by JAX's collectives and lax.ppermute only.
A program may use at most 128 MiB of HBM per device.

v0:
```python
import jax
import jax.numpy as jnp
from jax import lax
from jax.sharding import PartitionSpec as P

INNER = 1536
SPAN = 256
EPS = 1e-05


def silu_grad(values):
    sigmoid_of = jax.nn.sigmoid(values)
    return sigmoid_of * (1.0 + values * (1.0 - sigmoid_of))


def lagged(values, offset):
    if offset == 0:
        return values
    padding = jnp.zeros((offset,) + values.shape[1:], values.dtype)
    return jnp.concatenate([padding, values[:-offset]], 0)


def leading(values, offset):
    padding = jnp.zeros((offset,) + values.shape[1:], values.dtype)
    return jnp.concatenate([values[offset:], padding], 0)


def conv_apply(values, weight, bias, conv_masks):
    total = bias + weight[0] * values
    for offset in range(1, len(conv_masks)):
        total = total + weight[offset] * lagged(values, offset) * conv_masks[offset]
    return total


def conv_back(values, weight, conv_masks, grad_pre):
    grad_weight = jnp.stack(
        [
            jnp.sum(grad_pre * conv_masks[offset] * lagged(values, offset), 0)
            for offset in range(len(conv_masks))
        ],
        0,
    )
    grad_bias = jnp.sum(grad_pre, 0)
    grad_values = grad_pre * weight[0]
    for offset in range(1, len(conv_masks)):
        grad_values = grad_values + leading(grad_pre * conv_masks[offset], offset) * weight[offset]
    return (grad_weight, grad_bias, grad_values)


def per_device(
    hidden,
    cotangent,
    seg_ids,
    counts,
    norm_gain,
    w_x,
    w_z,
    w_dt,
    w_bc,
    conv_x,
    conv_x_bias,
    conv_bc,
    conv_bc_bias,
    dt_bias,
    a_log,
    d_skip,
    gate_gain,
    w_out,
):
    row_count = hidden.shape[0]
    state_width = w_bc.shape[1] // 2
    heads_here = w_dt.shape[1]
    width_here = w_x.shape[1]
    head_size = width_here // heads_here
    tap_count = conv_x.shape[0]
    span_count = row_count // SPAN
    highest = lax.Precision.HIGHEST
    positions = jnp.arange(row_count)
    live_rows = (positions < counts[0]).astype(jnp.float32)[:, None]
    conv_masks = [
        ((lagged(seg_ids, offset) == seg_ids) & (positions >= offset)).astype(jnp.float32)[:, None]
        for offset in range(tap_count)
    ]
    hidden_wide = hidden.astype(jnp.float32)
    inv_rms = lax.rsqrt(jnp.mean(hidden_wide * hidden_wide, -1, keepdims=True) + EPS)
    normed = (hidden_wide * inv_rms * norm_gain).astype(jnp.bfloat16)
    normed_wide = normed.astype(jnp.float32)
    proj_x = jnp.dot(normed, w_x, preferred_element_type=jnp.float32)
    proj_z = jnp.dot(normed, w_z, preferred_element_type=jnp.float32)
    proj_dt = jnp.dot(normed, w_dt, preferred_element_type=jnp.float32)
    proj_bc = jnp.dot(normed, w_bc, preferred_element_type=jnp.float32)
    x_pre = conv_apply(proj_x, conv_x, conv_x_bias, conv_masks)
    bc_pre = conv_apply(proj_bc, conv_bc, conv_bc_bias, conv_masks)
    x_conv = jax.nn.silu(x_pre)
    bc_conv = jax.nn.silu(bc_pre)
    b_low = bc_conv[:, :state_width].astype(jnp.bfloat16)
    c_low = bc_conv[:, state_width:].astype(jnp.bfloat16)
    dt_in = proj_dt + dt_bias
    step_size = jax.nn.softplus(dt_in)
    rates = -jnp.exp(a_log)
    log_decay = jnp.cumsum(step_size * rates, 0)
    x_heads = x_conv.reshape(row_count, heads_here, head_size)
    inputs = (step_size[:, :, None] * x_heads).astype(jnp.bfloat16)
    ld_blocks = log_decay.reshape(span_count, SPAN, heads_here)
    seg_blocks = seg_ids.reshape(span_count, SPAN)
    local_pos = jnp.arange(SPAN)
    intra = (local_pos[:, None] >= local_pos[None, :])[None] & (
        seg_blocks[:, :, None] == seg_blocks[:, None, :]
    )
    ld_heads = jnp.transpose(ld_blocks, (0, 2, 1))
    exponent = jnp.where(
        intra[:, None], ld_heads[:, :, :, None] - ld_heads[:, :, None, :], -10000.0
    )
    decays = jnp.exp(exponent)
    b_blocks = b_low.reshape(span_count, SPAN, state_width)
    c_blocks = c_low.reshape(span_count, SPAN, state_width)
    inputs_blocks = inputs.reshape(span_count, SPAN, heads_here, head_size)
    kernel = jnp.einsum("cpn,cqn->cpq", c_blocks, b_blocks, preferred_element_type=jnp.float32)
    mixing = (kernel[:, None] * decays).astype(jnp.bfloat16)
    local_part = jnp.einsum(
        "chpq,cqhd->cphd", mixing, inputs_blocks, preferred_element_type=jnp.float32
    )
    ld_end = ld_blocks[:, -1]
    seg_end = seg_blocks[:, -1]
    in_keep = (seg_blocks == seg_end[:, None])[:, :, None]
    decay_in = jnp.where(in_keep, jnp.exp(ld_end[:, None, :] - ld_blocks), 0.0)
    b_blocks_wide = b_blocks.astype(jnp.float32)
    weighted_b = (b_blocks_wide[:, :, None, :] * decay_in[..., None]).astype(jnp.bfloat16)
    span_new = jnp.einsum(
        "cqhn,cqhd->chnd", weighted_b, inputs_blocks, preferred_element_type=jnp.float32
    )
    hop = jnp.where((seg_end[1:] == seg_end[:-1])[:, None], jnp.exp(ld_end[1:] - ld_end[:-1]), 0.0)
    state = jnp.zeros((heads_here, state_width, head_size), jnp.float32)
    befores = []
    for span in range(span_count):
        befores.append(state)
        if span == 0:
            state = span_new[0]
        else:
            state = hop[span - 1][:, None, None] * state + span_new[span]
    states_before = jnp.stack(befores, 0)
    carried_low = states_before.astype(jnp.bfloat16)
    prev_seg = jnp.concatenate([jnp.full((1,), -1, jnp.int32), seg_end[:-1]], 0)
    prev_ld = jnp.concatenate([jnp.zeros((1, heads_here), jnp.float32), ld_end[:-1]], 0)
    out_keep = (seg_blocks == prev_seg[:, None])[:, :, None]
    decay_out = jnp.where(out_keep, jnp.exp(ld_blocks - prev_ld[:, None, :]), 0.0)
    cross_raw = jnp.einsum(
        "cpn,chnd->cphd", c_blocks, carried_low, preferred_element_type=jnp.float32
    )
    scanned = (local_part + decay_out[..., None] * cross_raw).reshape(
        row_count, heads_here, head_size
    )
    y_flat = (scanned + d_skip[None, :, None] * x_heads).reshape(row_count, width_here)
    z_active = jax.nn.silu(proj_z)
    gated_out = y_flat * z_active
    squares = lax.psum(jnp.sum(gated_out * gated_out, -1), "tensor")
    inv_gate = lax.rsqrt(squares[:, None] / INNER + EPS)
    scaled = gated_out * inv_gate
    out_in = (scaled * gate_gain).astype(jnp.bfloat16)
    mixed = lax.psum(jnp.dot(out_in, w_out, preferred_element_type=jnp.float32), "tensor")
    output = (hidden_wide + live_rows * mixed).astype(jnp.bfloat16)
    grad_out = cotangent.astype(jnp.float32)
    grad_mix = (live_rows * grad_out).astype(jnp.bfloat16)
    grad_w_out = jnp.dot(out_in.T, grad_mix, preferred_element_type=jnp.float32)
    grad_in = jnp.dot(grad_mix, w_out.T, preferred_element_type=jnp.float32)
    grad_gate_gain = jnp.sum(grad_in * scaled, 0)
    grad_scaled = grad_in * gate_gain
    cross_sum = lax.psum(jnp.sum(grad_scaled * gated_out, -1), "tensor")
    grad_gated = inv_gate * grad_scaled - gated_out * inv_gate**3 * cross_sum[:, None] / INNER
    grad_y = (grad_gated * z_active).reshape(row_count, heads_here, head_size)
    grad_z = (grad_gated * y_flat * silu_grad(proj_z)).astype(jnp.bfloat16)
    grad_d_skip = jnp.sum(grad_y * x_heads, (0, 2))
    grad_scan = grad_y.astype(jnp.bfloat16)
    grad_scan_blocks = grad_scan.reshape(span_count, SPAN, heads_here, head_size)
    grad_mixing = jnp.einsum(
        "cphd,cqhd->chpq", grad_scan_blocks, inputs_blocks, preferred_element_type=jnp.float32
    )
    grad_inputs_blocks = jnp.einsum(
        "chpq,cphd->cqhd", mixing, grad_scan_blocks, preferred_element_type=jnp.float32
    )
    grad_kernel = (grad_mixing * decays).astype(jnp.bfloat16)
    grad_expo = grad_mixing * kernel[:, None] * decays
    grad_ld = jnp.transpose(jnp.sum(grad_expo, 3) - jnp.sum(grad_expo, 2), (0, 2, 1))
    grad_c_blocks = jnp.einsum(
        "chpq,cqn->cpn", grad_kernel, b_blocks, preferred_element_type=jnp.float32
    )
    grad_b_blocks = jnp.einsum(
        "chpq,cpn->cqn", grad_kernel, c_blocks, preferred_element_type=jnp.float32
    )
    grad_scan_wide = grad_scan_blocks.astype(jnp.float32)
    grad_decay_out = jnp.sum(grad_scan_wide * cross_raw, -1)
    grad_cross_raw = decay_out[..., None] * grad_scan_wide
    grad_c_blocks = grad_c_blocks + jnp.einsum(
        "cphd,chnd->cpn",
        grad_cross_raw,
        carried_low.astype(jnp.float32),
        precision=highest,
        preferred_element_type=jnp.float32,
    )
    grad_states = jnp.einsum(
        "cpn,cphd->chnd",
        c_blocks.astype(jnp.float32),
        grad_cross_raw,
        precision=highest,
        preferred_element_type=jnp.float32,
    )
    out_term = grad_decay_out * decay_out
    grad_ld = grad_ld + out_term
    grad_prev_ld = -jnp.sum(out_term, 1)
    grad_end = jnp.concatenate([grad_prev_ld[1:], jnp.zeros((1, heads_here), jnp.float32)], 0)
    flow = jnp.zeros((heads_here, state_width, head_size), jnp.float32)
    grad_new_list = [flow] * span_count
    hop_grads = []
    for span in reversed(range(span_count)):
        grad_new_list[span] = flow
        if span > 0:
            hop_grads.append(jnp.sum(flow * states_before[span], (1, 2)))
            flow = grad_states[span] + hop[span - 1][:, None, None] * flow
    grad_new = jnp.stack(grad_new_list, 0)
    hop_terms = jnp.stack(hop_grads[::-1], 0) * hop
    zero_row = jnp.zeros((1, heads_here), jnp.float32)
    grad_end = (
        grad_end
        + jnp.concatenate([zero_row, hop_terms], 0)
        - jnp.concatenate([hop_terms, zero_row], 0)
    )
    grad_weighted_b = jnp.einsum(
        "chnd,cqhd->cqhn",
        grad_new,
        inputs_blocks.astype(jnp.float32),
        precision=highest,
        preferred_element_type=jnp.float32,
    )
    grad_inputs_blocks = grad_inputs_blocks + jnp.einsum(
        "chnd,cqhn->cqhd",
        grad_new,
        weighted_b.astype(jnp.float32),
        precision=highest,
        preferred_element_type=jnp.float32,
    )
    grad_b_blocks = grad_b_blocks + jnp.sum(grad_weighted_b * decay_in[..., None], 2)
    in_term = jnp.sum(grad_weighted_b * b_blocks_wide[:, :, None, :], -1) * decay_in
    grad_end = grad_end + jnp.sum(in_term, 1)
    grad_ld = grad_ld - in_term
    end_mask = (local_pos == SPAN - 1).astype(jnp.float32)[None, :, None]
    grad_ld = grad_ld + end_mask * grad_end[:, None, :]
    grad_log = grad_ld.reshape(row_count, heads_here)
    grad_rate_sum = jnp.cumsum(grad_log[::-1], 0)[::-1]
    grad_inputs = grad_inputs_blocks.reshape(row_count, heads_here, head_size)
    grad_step = jnp.sum(grad_inputs * x_heads, -1) + grad_rate_sum * rates
    grad_a_log = jnp.sum(grad_rate_sum * step_size, 0) * rates
    grad_dt_in = grad_step * jax.nn.sigmoid(dt_in)
    grad_dt_bias = jnp.sum(grad_dt_in, 0)
    grad_x_heads = grad_y * d_skip[None, :, None] + grad_inputs * step_size[:, :, None]
    grad_bc = jnp.concatenate(
        [
            grad_b_blocks.reshape(row_count, state_width),
            grad_c_blocks.reshape(row_count, state_width),
        ],
        1,
    )
    grad_x_pre = grad_x_heads.reshape(row_count, width_here) * silu_grad(x_pre)
    grad_conv_x, grad_conv_x_bias, grad_proj_x = conv_back(proj_x, conv_x, conv_masks, grad_x_pre)
    grad_proj_low = grad_proj_x.astype(jnp.bfloat16)
    grad_w_x = jnp.dot(normed.T, grad_proj_low, preferred_element_type=jnp.float32)
    grad_w_z = jnp.dot(normed.T, grad_z, preferred_element_type=jnp.float32)
    grad_w_dt = jnp.dot(
        normed_wide.T, grad_dt_in, precision=highest, preferred_element_type=jnp.float32
    )
    partial_in = (
        jnp.dot(grad_proj_low, w_x.T, preferred_element_type=jnp.float32)
        + jnp.dot(grad_z, w_z.T, preferred_element_type=jnp.float32)
        + jnp.dot(
            grad_dt_in,
            w_dt.astype(jnp.float32).T,
            precision=highest,
            preferred_element_type=jnp.float32,
        )
    )
    bc_total = lax.psum(grad_bc, "tensor")
    grad_bc_pre = bc_total * silu_grad(bc_pre)
    grad_conv_bc, grad_conv_bc_bias, grad_proj_bc = conv_back(
        proj_bc, conv_bc, conv_masks, grad_bc_pre
    )
    grad_w_bc = jnp.dot(
        normed_wide.T, grad_proj_bc, precision=highest, preferred_element_type=jnp.float32
    )
    from_state = jnp.dot(
        grad_proj_bc,
        w_bc.astype(jnp.float32).T,
        precision=highest,
        preferred_element_type=jnp.float32,
    )
    summed_in = lax.psum(partial_in, "tensor")
    grad_normed = summed_in + from_state
    weighted = grad_normed * norm_gain
    grad_norm_gain = jnp.sum(grad_normed * hidden_wide * inv_rms, 0)
    grad_hidden = (
        grad_out
        + inv_rms * weighted
        - hidden_wide * inv_rms**3 * jnp.mean(weighted * hidden_wide, -1, keepdims=True)
    )
    main_sums = lax.psum(
        (
            grad_norm_gain,
            grad_w_x,
            grad_w_z,
            grad_w_dt,
            grad_conv_x,
            grad_conv_x_bias,
            grad_dt_bias,
            grad_a_log,
            grad_d_skip,
            grad_gate_gain,
            grad_w_out,
        ),
        "dp",
    )
    state_sums = lax.psum((grad_w_bc, grad_conv_bc, grad_conv_bc_bias), "dp")
    return (
        output,
        grad_hidden,
        main_sums[0],
        main_sums[1],
        main_sums[2],
        main_sums[3],
        state_sums[0],
        main_sums[4],
        main_sums[5],
        state_sums[1],
        state_sums[2],
        main_sums[6],
        main_sums[7],
        main_sums[8],
        main_sums[9],
        main_sums[10],
    )


def solution(mesh):
    return jax.shard_map(
        per_device,
        mesh=mesh,
        in_specs=(
            P("dp", None),
            P("dp", None),
            P("dp"),
            P("dp"),
            P(),
            P(None, "tensor"),
            P(None, "tensor"),
            P(None, "tensor"),
            P(),
            P(None, "tensor"),
            P("tensor"),
            P(),
            P(),
            P("tensor"),
            P("tensor"),
            P("tensor"),
            P("tensor"),
            P("tensor", None),
        ),
        out_specs=(
            P("dp", None),
            P("dp", None),
            P(),
            P(None, "tensor"),
            P(None, "tensor"),
            P(None, "tensor"),
            P(),
            P(None, "tensor"),
            P("tensor"),
            P(),
            P(),
            P("tensor"),
            P("tensor"),
            P("tensor"),
            P("tensor"),
            P("tensor", None),
        ),
        check_vma=False,
    )
```

profile of v0, /device:TPU:0, one launch (start us, length us, event | category | flops | bytes accessed | tf_op | source)
XLA Modules:
  0.0 647.3 jit_solution(8219857742431929211)
XLA Ops:
  7.3 2.7 fusion.6
  12.0 1.7 copy-done.3
  14.8 2.0 reduce-window.14
  20.3 3.7 fusion.94
  24.3 4.9 fusion.37
  29.2 3.6 copy.189
  32.7 5.2 copy.238
  39.1 3.4 multiply_convert_fusion.10
  43.5 2.2 copy.195
  46.6 1.6 fusion.96
  48.9 1.4 copy-done.26
  50.2 1.2 fusion.27
  53.5 5.2 bitcast_add_fusion.1
  58.8 1.8 copy.203
  60.6 3.1 copy.242
  63.6 3.5 copy.204
  67.3 9.4 %multiply_reduce_fusion.7 = (f32[2048]{0:T(1024)S(1)}, f32[2048,384]{1,0:T(8,128)}, f32[2048,384]{1,0:T(8,128)}) fusion(f32[2048,384]{1,0:T(8,128)} %copy.204, f32[2048,384]{1,0:T(8,128)} %get-tuple-element.98, f32[384]{0:T(512)S(1)} %mul.880, bf16[2048,768]{1,0:T(8,128)(2,1)} %copy-done.3, bf16[768,384]{1,0:T(8,128)(2,1)S(1)} %copy-done), kind=kOutput, calls=%fused_computation.67 | convolution fusion | flops 1218181120 | bytes 16328192 | tf_op jit(solution)/shard_map/dot_general | solution.py:89
  76.7 8.5 %psum.133 = f32[2048]{0:T(1024)S(1)} all-reduce(f32[2048]{0:T(1024)S(1)} %get-tuple-element.89), channel_id=1, replica_groups=mesh['dp'=8,'tensor'=4] {'tensor'}, use_global_device_ids=true, to_apply=%region_4.5 | all-reduce | flops 2048 | bytes 16384 | tf_op jit(solution)/shard_map/psum | solution.py:156
  85.9 7.4 %multiply_reduce_fusion = (f32[384]{0:T(512)}, f32[2048]{0:T(1024)S(1)}, f32[2048,384]{1,0:T(8,128)}) fusion(f32[2048,384]{1,0:T(8,128)} %get-tuple-element.90, f32[2048]{0:T(1024)S(1)} %get-tuple-element.122, f32[384]{0:T(512)S(1)} %copy-done.70, bf16[384,768]{1,0:T(8,128)(2,1)} %param.35, bf16[2048,768]{1,0:T(8,128)(2,1)} %param.19, f32[2048]{0:T(1024)S(1)} %fusion.72), kind=kOutput, calls=%fused_computation.55 | convolution fusion | flops 1217394304 | bytes 10054656 | tf_op jit(solution)/shard_map/dot_general | solution.py:165
  93.3 5.8 psum.135
  99.2 9.2 %multiply_reduce_fusion.1 = (f32[384]{0:T(512)}, f32[2048,384]{1,0:T(8,128)S(1)}, bf16[2048,384]{1,0:T(8,128)(2,1)}) fusion(f32[2048,384]{1,0:T(8,128)} %get-tuple-element.98, f32[2048,384]{1,0:T(8,128)} %get-tuple-element.136, f32[2048]{0:T(1024)S(1)} %psum.135, f32[2048,384]{1,0:T(8,128)} %get-tuple-element.90, f32[2048]{0:T(1024)S(1)} %get-tuple-element.121, ...), kind=kLoop, calls=%fused_computation.56 | loop fusion | flops 20446848 | bytes 20476416 | tf_op jit(solution)/shard_map/reduce_sum | solution.py:172
  108.4 1.6 copy-done.12
  110.0 1.3 convert_element_type.108
  111.3 2.6 copy.205
  113.9 2.0 copy.243
  116.1 9.8 %fusion = (f32[8,6,256]{2,1,0:T(8,128)}, f32[8,6,256]{2,1,0:T(8,128)}, bf16[8,256,256]{2,1,0:T(8,128)(2,1)}) fusion(f32[8,6,256]{2,1,0:T(8,128)S(1)} %copy.190, f32[8,256,256]{2,1,0:T(8,128)S(1)} %copy-done.31, pred[8,256,256]{2,1,0:T(8,128)(4,1)S(1)} %copy-done.55, bf16[8,256,6,64]{1,0,3,2:T(8,128)(2,1)} %copy-done.34, ...), kind=kOutput, calls=%fused_computation.11 | convolution fusion | flops 433561600 | bytes 6963200 | tf_op jit(solution)/shard_map/cphd,cqhd->chpq/dot_general | solution.py:175
  125.9 3.7 fusion.42
  129.6 1.8 fusion.41
  131.7 1.5 multiply_reduce_fusion.13
  133.2 1.3 fusion.30
  135.1 4.8 fusion.2
  140.0 4.5 fusion.85
  144.9 4.7 fusion.15
  149.6 2.6 copy.227
  152.2 3.2 convolution_add_fusion.3
  155.5 1.4 convolution_add_fusion.2
  160.0 1.7 reduce-window.16
  162.2 1.5 rev.7
  163.7 6.3 fusion.31
  170.0 1.8 copy.209
  171.8 3.1 copy.244
  174.9 3.6 copy.210
  178.5 2.0 mul.911
  180.6 3.6 copy.211
  184.2 6.5 %fusion.86 = (f32[384]{0:T(512)S(1)}, f32[384]{0:T(512)S(1)}, f32[2048,384]{1,0:T(8,128)S(1)}) fusion(f32[2048,384]{1,0:T(8,128)} %copy-done.1, f32[2048,384]{1,0:T(8,128)} %get-tuple-element.98, f32[2048,384]{1,0:T(8,128)} %copy.210, f32[2048,384]{1,0:T(8,128)} %copy.211, f32[2048,384]{1,0:T(8,128)} %copy-done.12, f32[384]{0:T(512)S(1)} %copy-done.101), kind=kLoop, calls=%fused_computation.247 | loop fusion | flops 11009280 | bytes 18878976 | tf_op jit(solution)/shard_map/reduce_sum | solution.py:43
  190.7 2.8 multiply_reduce_fusion.4
  195.7 1.8 fusion.98
  197.7 1.8 fusion.99
  199.5 1.5 pad_maximum_fusion
  201.3 4.7 add_add_fusion
  206.1 5.3 fusion.100
  211.4 2.8 fusion.101
  214.3 2.8 fusion.43
  217.1 244.0 %all-reduce.26.cloned.1.call-done = (f32[2048,768]{1,0:T(8,128)}, f32[2048,768]{1,0:T(8,128)}, f32[2048,256]{1,0:T(8,128)}) async-done(((f32[2048,768]{1,0:T(8,128)}, f32[2048,768]{1,0:T(8,128)}, f32[2048,256]{1,0:T(8,128)}), (f32[2048,768]{1,0:T(8,128)}, f32[2048,768]{1,0:T(8,128)}, f32[2048,256]{1,0:T(8,128)})) %all-reduce.26.cloned.1.call-update) | async-done | bytes 14680080 | tf_op jit(solution)/shard_map/psum | solution.py:160
  461.2 3.1 fusion.87
  464.3 2.1 multiply_reduce_fusion.10
  468.0 1.3 copy-done.6
  469.3 4.5 fusion.103
  474.7 3.3 fusion.102
  478.1 8.3 %fusion.13 = (f32[768]{0:T(1024)S(1)}, f32[2048]{0:T(1024)S(1)}, f32[2048,768]{1,0:T(8,128)}) fusion(bf16[2048,768]{1,0:T(8,128)(2,1)S(1)} %copy-done.8, f32[2048]{0:T(1024)S(1)} %copy-done.67, f32[768]{0:T(1024)S(1)} %copy-done.78, f32[2048,768]{1,0:T(8,128)} %get-tuple-element.61, f32[2048,256]{1,0:T(8,128)S(1)} %multiply_add_fusion.2, ...), kind=kOutput, calls=%fused_computation.26 | convolution fusion | flops 4844418048 | bytes 18241536 | tf_op jit(solution)/shard_map/dot_general | solution.py:288
  486.5 40.8 %all-reduce.18 = (f32[768]{0:T(1024)}, f32[768,6]{0,1:T(8,128)}, f32[4,384]{1,0:T(4,128)}, f32[384]{0:T(512)}, f32[4,256]{1,0:T(4,128)}, /*index=5*/f32[256]{0:T...) all-reduce(f32[768]{0:T(1024)S(1)} %get-tuple-element.19, ...), channel_id=1, replica_groups=mesh['dp'=8,'tensor'=4] {'dp'}, use_global_device_ids=true, to_apply=%region_30.31 | all-reduce | flops 8978 | bytes 71824 | tf_op jit(solution)/shard_map/psum | solution.py:303
  527.3 11.3 %fusion.5 = (f32[2048,768]{1,0:T(8,128)}, bf16[2048,768]{1,0:T(8,128)(2,1)}) fusion(bf16[2048,768]{1,0:T(8,128)(2,1)} %param.19, bf16[2048,768]{1,0:T(8,128)(2,1)} %param.18, f32[2048,768]{1,0:T(8,128)} %get-tuple-element.140, f32[2048]{0:T(1024)S(1)} %broadcast_multiply_fusion.6, f32[2048]{0:T(1024)S(1)} %copy-done.79, f32[768]{0:T(1024)S(1)} %copy-done.78, ...), kind=kLoop, calls=%fused_computation.18 | loop fusion | flops 17301504 | bytes 28347392 | tf_op jit(solution)/shard_map/sub | solution.py:299
  538.6 96.2 %all-reduce.24.cloned.1.call-done = (f32[768,384]{1,0:T(8,128)}, f32[768,384]{1,0:T(8,128)}, f32[768,256]{1,0:T(8,128)}, f32[384,768]{1,0:T(8,128)}) async-done(((f32[768,384]{1,0:T(8,128)}, f32[768,384]{1,0:T(8,128)}, f32[768,256]{1,0:T(8,128)}, f32[384,768]{1,0:T(8,128)}), (f32[768,384]{1,0:T(8,128)}, f32[768,384]{1,0:T(8,128)}, f32[768,256]{1,0:T(8,128)}, ...) | async-done | bytes 4325392 | tf_op jit(solution)/shard_map/psum | solution.py:303
  634.8 2.5 copy.314
  (369 shorter events, 24.9 us)
Async XLA Ops:
  7.2 60.1 %copy-start = (bf16[768,384]{1,0:T(8,128)(2,1)S(1)}, bf16[768,384]{1,0:T(8,128)(2,1)}, u32[]{:S(2)}) copy-start(bf16[768,384]{1,0:T(8,128)(2,1)} %param.24) | copy-start | bytes 1769476
  7.2 4.0 copy-start.77
  7.2 453.9 %all-reduce.26.cloned.1.call-start = ((), (), s32[]{:S(2)}) async-start(), calls=%async_computation.1 | async-start | bytes 29360128 | tf_op jit(solution)/shard_map/psum | solution.py:160
  10.6 4.0 copy-start.121
  13.7 6.6 %copy-start.52 = (bf16[768,384]{1,0:T(8,128)(2,1)S(1)}, bf16[768,384]{1,0:T(8,128)(2,1)}, u32[]{:S(2)}) copy-start(bf16[768,384]{1,0:T(8,128)(2,1)} %param.23) | copy-start | bytes 1769476
  14.6 9.4 %copy-start.46 = (f32[2048,6]{0,1:T(8,128)}, f32[2048,6]{0,1:T(8,128)S(1)}, u32[]{:S(2)}) copy-start(f32[2048,6]{0,1:T(8,128)S(1)} %get-tuple-element.135) | copy-start | bytes 147460
  14.7 23.3 %copy-start.44 = (f32[2048,6]{0,1:T(8,128)}, f32[2048,6]{0,1:T(8,128)S(1)}, u32[]{:S(2)}) copy-start(f32[2048,6]{0,1:T(8,128)S(1)} %get-tuple-element.134) | copy-start | bytes 147460
  24.1 5.1 copy-start.1
  24.1 5.0 copy-start.86
  24.1 5.0 copy-start.88
  24.1 5.0 copy-start.90
  24.1 5.0 copy-start.92
  24.2 14.8 %copy-start.58 = (f32[2048]{0:T(1024)}, f32[2048]{0:T(1024)S(1)}, u32[]{:S(2)}) copy-start(f32[2048]{0:T(1024)S(1)} %get-tuple-element.125) | copy-start | bytes 24580
  24.2 14.8 %copy-start.60 = (f32[2048]{0:T(1024)}, f32[2048]{0:T(1024)S(1)}, u32[]{:S(2)}) copy-start(f32[2048]{0:T(1024)S(1)} %get-tuple-element.126) | copy-start | bytes 24580
  24.3 14.8 %copy-start.62 = (f32[2048]{0:T(1024)}, f32[2048]{0:T(1024)S(1)}, u32[]{:S(2)}) copy-start(f32[2048]{0:T(1024)S(1)} %get-tuple-element.127) | copy-start | bytes 24580
  32.7 5.2 copy-start.4
  32.7 5.2 copy-start.36
  46.6 5.0 copy-start.115
  46.6 5.2 copy-start.80
  46.6 5.2 copy-start.97
  46.6 5.5 copy-start.83
  46.6 5.5 copy-start.94
  46.6 5.6 copy-start.104
  48.2 5.3 copy-start.30
  48.7 4.8 copy-start.34
  52.9 5.9 copy-start.19
  52.9 63.0 %copy-start.73 = (f32[8,6,256]{2,1,0:T(8,128)}, f32[8,6,256]{2,1,0:T(8,128)S(1)}, u32[]{:S(2)}) copy-start(f32[8,6,256]{2,1,0:T(8,128)S(1)} %copy.190) | copy-start | bytes 147460
  53.5 5.3 copy-start.54
  67.3 31.8 %copy-start.100 = (f32[384]{0:T(512)}, f32[384]{0:T(512)S(1)}, u32[]{:S(2)}) copy-start(f32[384]{0:T(512)S(1)} %mul.880) | copy-start | bytes 4612
  67.3 18.6 %copy-start.70 = (f32[384]{0:T(512)S(1)}, f32[384]{0:T(512)}, u32[]{:S(2)}) copy-start(f32[384]{0:T(512)} %param.34) | copy-start | bytes 4612
  85.9 7.4 %copy-start.68 = (f32[2048]{0:T(1024)}, f32[2048]{0:T(1024)S(1)}, u32[]{:S(2)}) copy-start(f32[2048]{0:T(1024)S(1)} %fusion.72) | copy-start | bytes 24580
  116.1 9.8 %copy-start.43 = (bf16[8,6,128,64]{2,3,1,0:T(8,128)(2,1)S(1)}, bf16[8,6,128,64]{2,3,1,0:T(8,128)(2,1)}, u32[]{:S(2)}) copy-start(bf16[8,6,128,64]{2,3,1,0:T(8,128)(2,1)} %copy-done.42) | copy-start | bytes 2359300
  125.9 5.6 copy-start.81
  125.9 5.6 copy-start.84
  125.9 5.6 copy-start.95
  125.9 5.6 copy-start.98
  125.9 5.6 copy-start.102
  125.9 5.6 copy-start.105
  125.9 5.6 copy-start.116
  131.4 13.3 %copy-start.16 = (f32[8,6,128,64]{2,3,1,0:T(8,128)}, f32[8,6,128,64]{2,3,1,0:T(8,128)S(1)}, u32[]{:S(2)}) copy-start(f32[8,6,128,64]{2,3,1,0:T(8,128)S(1)} %fusion.41) | copy-start | bytes 4718596
  135.1 4.8 copy-start.9
  135.1 4.9 copy-start.51
  139.9 4.9 copy-start.27
  140.0 4.9 copy-start.35
  144.9 4.7 copy-start.32
  152.2 4.7 copy-start.17
  152.2 4.7 copy-start.23
  152.2 4.7 copy-start.33
  152.2 4.7 copy-start.85
  152.2 4.7 copy-start.96
  184.1 6.5 %copy-start.2 = (f32[2048,384]{1,0:T(8,128)S(1)}, f32[2048,384]{1,0:T(8,128)}, u32[]{:S(2)}) copy-start(f32[2048,384]{1,0:T(8,128)} %copy-done.1) | copy-start | bytes 9437188
  184.1 6.5 %copy-start.59 = (f32[2048]{0:T(1024)S(1)}, f32[2048]{0:T(1024)}, u32[]{:S(2)}) copy-start(f32[2048]{0:T(1024)} %copy-done.58) | copy-start | bytes 24580
  184.1 6.5 %copy-start.61 = (f32[2048]{0:T(1024)S(1)}, f32[2048]{0:T(1024)}, u32[]{:S(2)}) copy-start(f32[2048]{0:T(1024)} %copy-done.60) | copy-start | bytes 24580
  184.2 6.5 %copy-start.63 = (f32[2048]{0:T(1024)S(1)}, f32[2048]{0:T(1024)}, u32[]{:S(2)}) copy-start(f32[2048]{0:T(1024)} %copy-done.62) | copy-start | bytes 24580
  206.0 428.8 %all-reduce.24.cloned.1.call-start = ((), (), s32[]{:S(2)}) async-start(), calls=%async_computation | async-start | bytes 8650752 | tf_op jit(solution)/shard_map/psum | solution.py:303
  206.1 5.4 copy-start.5
  206.1 5.4 copy-start.14
  206.1 8.2 %copy-start.18 = (bf16[2048,768]{1,0:T(8,128)(2,1)S(1)}, bf16[2048,768]{1,0:T(8,128)(2,1)}, u32[]{:S(2)}) copy-start(bf16[2048,768]{1,0:T(8,128)(2,1)} %param.19) | copy-start | bytes 9437188
  473.8 4.3 copy-start.37
  473.8 4.3 copy-start.67
  473.8 4.3 copy-start.78
  478.1 8.4 %copy-start.124 = (f32[384]{0:T(512)S(1)}, f32[384]{0:T(512)}, u32[]{:S(2)}) copy-start(f32[384]{0:T(512)} %get-tuple-element.21) | copy-start | bytes 4612
  478.1 49.2 %copy-start.79 = (f32[2048]{0:T(1024)S(1)}, f32[2048]{0:T(1024)}, u32[]{:S(2)}) copy-start(f32[2048]{0:T(1024)} %get-tuple-element.119) | copy-start | bytes 24580
  634.8 4.4 copy-start.38
  (69 other events, 153.5 us)
Sparse Core Ops, SparseCore 0:
  206.1 254.9 all-reduce.25
  473.9 160.7 all-reduce.23
where the time goes:
time: 650 us; the launch traced here: 647 us
  waiting for transfers between devices  340 us (52%)
  matrix products  107 us (16%)
  other arithmetic  64.3 us (10%)
  local copies, waits for them, and re-layouts  64 us (10%)
  blocking collectives  55.2 us (8%)
  between operations  16.7 us (3%)
    psum x1, waiting for transfers between devices, per_device(): lax.psum(jnp.dot(out_in, w_out, preferred_element_type=jnp.float32), 'ten...  244 us
    psum x1, waiting for transfers between devices, per_device(): lax.psum((grad_norm_gain, grad_w_x, grad_w_z, grad_w_dt, grad_conv_x, gra...  96.2 us
    psum x1, blocking collectives, per_device(): lax.psum((grad_norm_gain, grad_w_x, grad_w_z, grad_w_dt, grad_conv_x, gra...  40.8 us
    unnamed x284, local copies, waits for them, and re-layouts  29.5 us
  transfers between devices with their start and end apart: 2, of which 2 were waited for; matrix products, arithmetic and copies ran while one was open for 5% of the time, Pallas kernels for 0%

commit v1 on v0

--- a/solution.py
+++ b/solution.py
@@ -157,7 +157,9 @@
     inv_gate = lax.rsqrt(squares[:, None] / INNER + EPS)
     scaled = gated_out * inv_gate
     out_in = (scaled * gate_gain).astype(jnp.bfloat16)
-    mixed = lax.psum(jnp.dot(out_in, w_out, preferred_element_type=jnp.float32), "tensor")
+    mixed = jnp.sum(
+        lax.all_gather(jnp.dot(out_in, w_out, preferred_element_type=jnp.float32), "tensor"), axis=0
+    )
     output = (hidden_wide + live_rows * mixed).astype(jnp.bfloat16)
     grad_out = cotangent.astype(jnp.float32)
     grad_mix = (live_rows * grad_out).astype(jnp.bfloat16)

time: 650 us -> 691 us (1.063)
  waiting for transfers between devices: 340 us -> 368 us
  other arithmetic: 64.3 us -> 76.9 us
    psum x1, waiting for transfers between devices: 244 us -> 136 us  [per_device(): summed_in = lax.psum(partial_in, 'tensor')]
    all_gather x0 -> x1, waiting for transfers between devices: none -> 91.5 us  [per_device(): lax.all_gather(jnp.dot(out_in, w_out, preferred_element_type=jnp.float32)...]
    psum x1, waiting for transfers between devices: 96.2 us -> 141 us  [per_device(): lax.psum((grad_norm_gain, grad_w_x, grad_w_z, grad_w_dt, grad_conv_x, gra...]
    reduce_sum x0 -> x1, other arithmetic: none -> 12.9 us  [per_device(): jnp.sum(lax.all_gather(jnp.dot(out_in, w_out, preferred_element_type=jnp....]
    unnamed x284 -> x280, local copies, waits for them, and re-layouts: 29.5 us -> 30 us
  transfers between devices with their start and end apart: 2 -> 3, of which waited for: 2 -> 3; matrix products, arithmetic and copies ran while one was open for 5% -> 10% of each run, Pallas kernels for 0% -> 0%
where the time goes in v1:
time: 691 us; the launch traced here: 688 us
  waiting for transfers between devices  368 us (53%)
  matrix products  111 us (16%)
  other arithmetic  76.9 us (11%)
  local copies, waits for them, and re-layouts  64 us (9%)
  blocking collectives  52.4 us (8%)
  between operations  16.3 us (2%)
    psum x1, waiting for transfers between devices, per_device(): lax.psum((grad_norm_gain, grad_w_x, grad_w_z, grad_w_dt, grad_conv_x, gra...  141 us
    psum x1, waiting for transfers between devices, per_device(): summed_in = lax.psum(partial_in, 'tensor')  136 us
    all_gather x1, waiting for transfers between devices, per_device(): lax.all_gather(jnp.dot(out_in, w_out, preferred_element_type=jnp.float32)...  91.5 us
    psum x1, blocking collectives, per_device(): lax.psum((grad_norm_gain, grad_w_x, grad_w_z, grad_w_dt, grad_conv_x, gra...  38.1 us
    unnamed x280, local copies, waits for them, and re-layouts  30 us
  transfers between devices with their start and end apart: 3, of which 3 were waited for; matrix products, arithmetic and copies ran while one was open for 10% of the time, Pallas kernels for 0%

profile of v1, /device:TPU:0, one launch (start us, length us, event | category | flops | bytes accessed | tf_op | source)
XLA Modules:
  0.0 688.0 jit_solution(16049821443330311347)
XLA Ops:
  7.3 2.7 fusion.6
  12.0 1.7 copy-done.3
  14.8 2.0 reduce-window.14
  20.3 3.7 fusion.94
  24.3 4.9 fusion.37
  29.2 3.6 copy.189
  32.8 5.2 copy.238
  39.1 3.4 multiply_convert_fusion.10
  43.4 2.2 copy.195
  46.5 1.6 fusion.96
  48.8 1.4 copy-done.25
  53.5 5.2 bitcast_add_fusion.1
  58.7 1.8 copy.203
  60.5 3.1 copy.242
  63.6 3.6 copy.204
  67.4 9.2 %multiply_reduce_fusion.7 = (f32[2048]{0:T(1024)S(1)}, f32[2048,384]{1,0:T(8,128)}, f32[2048,384]{1,0:T(8,128)}) fusion(f32[2048,384]{1,0:T(8,128)} %copy.204, f32[2048,384]{1,0:T(8,128)} %get-tuple-element.97, f32[384]{0:T(512)S(1)} %mul.880, bf16[2048,768]{1,0:T(8,128)(2,1)} %copy-done.3, bf16[768,384]{1,0:T(8,128)(2,1)S(1)} %copy-done), kind=kOutput, calls=%fused_computation.67 | convolution fusion | flops 1218181120 | bytes 16328192 | tf_op jit(solution)/shard_map/dot_general | solution.py:89
  76.6 8.5 %psum.126 = f32[2048]{0:T(1024)S(1)} all-reduce(f32[2048]{0:T(1024)S(1)} %get-tuple-element.88), channel_id=1, replica_groups=mesh['dp'=8,'tensor'=4] {'tensor'}, use_global_device_ids=true, to_apply=%region_4.5 | all-reduce | flops 2048 | bytes 16384 | tf_op jit(solution)/shard_map/psum | solution.py:156
  85.8 7.4 %multiply_reduce_fusion = (f32[384]{0:T(512)}, f32[2048]{0:T(1024)S(1)}, f32[2048,384]{1,0:T(8,128)}) fusion(f32[2048,384]{1,0:T(8,128)} %get-tuple-element.89, f32[2048]{0:T(1024)S(1)} %get-tuple-element.121, f32[384]{0:T(512)S(1)} %copy-done.68, bf16[384,768]{1,0:T(8,128)(2,1)} %param.35, bf16[2048,768]{1,0:T(8,128)(2,1)} %param.19, f32[2048]{0:T(1024)S(1)} %fusion.72), kind=kOutput, calls=%fused_computation.55 | convolution fusion | flops 1217394304 | bytes 10054656 | tf_op jit(solution)/shard_map/dot_general | solution.py:167
  93.2 5.8 psum.127
  99.1 9.2 %multiply_reduce_fusion.1 = (f32[384]{0:T(512)}, f32[2048,384]{1,0:T(8,128)S(1)}, bf16[2048,384]{1,0:T(8,128)(2,1)}) fusion(f32[2048,384]{1,0:T(8,128)} %get-tuple-element.97, f32[2048,384]{1,0:T(8,128)} %get-tuple-element.135, f32[2048]{0:T(1024)S(1)} %psum.127, f32[2048,384]{1,0:T(8,128)} %get-tuple-element.89, f32[2048]{0:T(1024)S(1)} %get-tuple-element.120, ...), kind=kLoop, calls=%fused_computation.56 | loop fusion | flops 20446848 | bytes 20476416 | tf_op jit(solution)/shard_map/reduce_sum | solution.py:174
  108.3 1.7 copy-done.11
  110.0 1.4 convert_element_type.108
  111.3 2.6 copy.205
  113.9 2.0 copy.243
  116.1 9.8 %fusion = (f32[8,6,256]{2,1,0:T(8,128)}, f32[8,6,256]{2,1,0:T(8,128)}, bf16[8,256,256]{2,1,0:T(8,128)(2,1)}) fusion(f32[8,6,256]{2,1,0:T(8,128)S(1)} %copy.190, f32[8,256,256]{2,1,0:T(8,128)S(1)} %copy-done.30, pred[8,256,256]{2,1,0:T(8,128)(4,1)S(1)} %copy-done.53, bf16[8,256,6,64]{1,0,3,2:T(8,128)(2,1)} %copy-done.33, ...), kind=kOutput, calls=%fused_computation.11 | convolution fusion | flops 433561600 | bytes 6963200 | tf_op jit(solution)/shard_map/cphd,cqhd->chpq/dot_general | solution.py:177
  125.9 3.7 fusion.42
  129.7 1.8 fusion.41
  131.7 1.5 multiply_reduce_fusion.13
  133.2 1.3 fusion.30
  135.1 4.6 fusion.2
  140.2 5.3 fusion.15
  145.5 2.5 copy.227
  148.0 3.2 convolution_add_fusion.3
  151.3 1.4 convolution_add_fusion.2
  155.8 1.7 reduce-window.16
  159.1 6.3 fusion.31
  165.4 1.8 copy.209
  167.2 3.0 copy.244
  170.3 3.6 copy.210
  173.9 2.0 mul.911
  175.9 3.5 copy.211
  179.5 6.5 fusion.86
  186.0 2.8 multiply_reduce_fusion.4
  191.0 1.8 fusion.98
  193.0 1.8 fusion.99
  194.9 1.5 pad_maximum_fusion
  196.6 4.7 add_add_fusion
  201.3 6.7 fusion.85
  208.2 5.3 fusion.100
  213.5 2.8 fusion.101
  216.4 2.8 fusion.43
  219.2 135.5 %all-reduce.26.cloned.1.call-done = (f32[2048,768]{1,0:T(8,128)}, f32[2048,256]{1,0:T(8,128)}) async-done(((f32[2048,768]{1,0:T(8,128)}, f32[2048,256]{1,0:T(8,128)}), (f32[2048,768]{1,0:T(8,128)}, f32[2048,256]{1,0:T(8,128)})) %all-reduce.26.cloned.1.call-update) | async-done | bytes 8388624 | tf_op jit(solution)/shard_map/psum | solution.py:296
  354.7 3.1 fusion.87
  357.9 2.1 multiply_reduce_fusion.10
  361.5 1.7 copy-done.6
  363.3 4.5 fusion.103
  368.7 3.9 fusion.102
  372.8 8.9 %fusion.13 = (f32[768]{0:T(1024)S(1)}, f32[2048]{0:T(1024)S(1)}, f32[2048,768]{1,0:T(8,128)}) fusion(bf16[2048,768]{1,0:T(8,128)(2,1)S(1)} %copy-done.8, f32[2048]{0:T(1024)S(1)} %copy-done.65, f32[768]{0:T(1024)S(1)} %copy-done.76, f32[2048,768]{1,0:T(8,128)} %get-tuple-element.60, f32[2048,256]{1,0:T(8,128)S(1)} %multiply_add_fusion.2, ...), kind=kOutput, calls=%fused_computation.26 | convolution fusion | flops 4844418048 | bytes 18241536 | tf_op jit(solution)/shard_map/dot_general | solution.py:290
  381.7 38.1 %all-reduce.18 = (f32[768]{0:T(1024)}, f32[768,6]{0,1:T(8,128)}, f32[4,384]{1,0:T(4,128)}, f32[384]{0:T(512)}, f32[4,256]{1,0:T(4,128)}, /*index=5*/f32[256]{0:T...) all-reduce(f32[768]{0:T(1024)S(1)} %get-tuple-element.19, ...), channel_id=1, replica_groups=mesh['dp'=8,'tensor'=4] {'dp'}, use_global_device_ids=true, to_apply=%region_30.31 | all-reduce | flops 8978 | bytes 71824 | tf_op jit(solution)/shard_map/psum | solution.py:305
  419.8 91.5 %all-gather.3.cloned.1.call-done = f32[8192,768]{1,0:T(8,128)} async-done(((f32[2048,768]{1,0:T(8,128)}), f32[8192,768]{1,0:T(8,128)}) %all-gather.3.cloned.1.call-update) | async-done | bytes 25165840 | tf_op jit(solution)/shard_map/all_gather | solution.py:161
  511.3 12.9 %reduce_sum.339 = f32[2048,768]{1,0:T(8,128)} reduce(f32[4,2048,768]{2,1,0:T(8,128)} %bitcast.275, f32[]{:T(128)} %constant.14.clone.1), dimensions={0}, to_apply=%region_5.6 | reduce | flops 4718592 | bytes 31457284 | tf_op jit(solution)/shard_map/reduce_sum | solution.py:160
  524.2 11.0 %fusion.5 = (f32[2048,768]{1,0:T(8,128)}, bf16[2048,768]{1,0:T(8,128)(2,1)}) fusion(bf16[2048,768]{1,0:T(8,128)(2,1)} %param.19, bf16[2048,768]{1,0:T(8,128)(2,1)} %param.18, f32[2048,768]{1,0:T(8,128)} %get-tuple-element.139, f32[2048]{0:T(1024)S(1)} %broadcast_multiply_fusion.6, f32[2048]{0:T(1024)S(1)} %copy-done.77, f32[768]{0:T(1024)S(1)} %copy-done.76, ...), kind=kLoop, calls=%fused_computation.18 | loop fusion | flops 17301504 | bytes 28347392 | tf_op jit(solution)/shard_map/sub | solution.py:301
  535.2 140.7 %all-reduce.24.cloned.1.call-done = (f32[768,384]{1,0:T(8,128)}, f32[768,384]{1,0:T(8,128)}, f32[768,256]{1,0:T(8,128)}, f32[384,768]{1,0:T(8,128)}) async-done(((f32[768,384]{1,0:T(8,128)}, f32[768,384]{1,0:T(8,128)}, f32[768,256]{1,0:T(8,128)}, f32[384,768]{1,0:T(8,128)}), (f32[768,384]{1,0:T(8,128)}, f32[768,384]{1,0:T(8,128)}, f32[768,256]{1,0:T(8,128)}, ...) | async-done | bytes 4325392 | tf_op jit(solution)/shard_map/psum | solution.py:305
  675.9 2.5 copy.313
  (369 shorter events, 27.3 us)
Async XLA Ops:
  7.2 60.2 %copy-start = (bf16[768,384]{1,0:T(8,128)(2,1)S(1)}, bf16[768,384]{1,0:T(8,128)(2,1)}, u32[]{:S(2)}) copy-start(bf16[768,384]{1,0:T(8,128)(2,1)} %param.24) | copy-start | bytes 1769476
  7.2 4.0 copy-start.75
  7.2 347.5 %all-reduce.26.cloned.1.call-start = ((), (), s32[]{:S(2)}) async-start(), calls=%async_computation.2 | async-start | bytes 16777216 | tf_op jit(solution)/shard_map/psum | solution.py:296
  10.6 4.0 copy-start.119
  13.7 6.6 copy-start.50
  14.6 9.4 %copy-start.45 = (f32[2048,6]{0,1:T(8,128)}, f32[2048,6]{0,1:T(8,128)S(1)}, u32[]{:S(2)}) copy-start(f32[2048,6]{0,1:T(8,128)S(1)} %get-tuple-element.134) | copy-start | bytes 147460
  14.7 23.3 %copy-start.43 = (f32[2048,6]{0,1:T(8,128)}, f32[2048,6]{0,1:T(8,128)S(1)}, u32[]{:S(2)}) copy-start(f32[2048,6]{0,1:T(8,128)S(1)} %get-tuple-element.133) | copy-start | bytes 147460
  24.1 5.1 copy-start.1
  24.1 5.1 copy-start.84
  24.1 5.0 copy-start.86
  24.1 5.0 copy-start.88
  24.2 5.0 copy-start.90
  24.3 14.8 %copy-start.56 = (f32[2048]{0:T(1024)}, f32[2048]{0:T(1024)S(1)}, u32[]{:S(2)}) copy-start(f32[2048]{0:T(1024)S(1)} %get-tuple-element.124) | copy-start | bytes 24580
  24.3 14.8 %copy-start.58 = (f32[2048]{0:T(1024)}, f32[2048]{0:T(1024)S(1)}, u32[]{:S(2)}) copy-start(f32[2048]{0:T(1024)S(1)} %get-tuple-element.125) | copy-start | bytes 24580
  24.3 14.8 %copy-start.60 = (f32[2048]{0:T(1024)}, f32[2048]{0:T(1024)S(1)}, u32[]{:S(2)}) copy-start(f32[2048]{0:T(1024)S(1)} %get-tuple-element.126) | copy-start | bytes 24580
  32.8 5.2 copy-start.4
  32.8 5.2 copy-start.35
  46.5 5.0 copy-start.113
  46.5 5.2 copy-start.78
  46.5 5.2 copy-start.95
  46.5 5.5 copy-start.81
  46.5 5.5 copy-start.92
  46.5 5.6 copy-start.102
  48.2 5.3 copy-start.29
  48.7 4.8 copy-start.33
  52.9 5.9 copy-start.18
  52.9 63.1 %copy-start.71 = (f32[8,6,256]{2,1,0:T(8,128)}, f32[8,6,256]{2,1,0:T(8,128)S(1)}, u32[]{:S(2)}) copy-start(f32[8,6,256]{2,1,0:T(8,128)S(1)} %copy.190) | copy-start | bytes 147460
  53.5 5.3 copy-start.52
  67.4 31.7 %copy-start.98 = (f32[384]{0:T(512)}, f32[384]{0:T(512)S(1)}, u32[]{:S(2)}) copy-start(f32[384]{0:T(512)S(1)} %mul.880) | copy-start | bytes 4612
  67.4 18.4 %copy-start.68 = (f32[384]{0:T(512)S(1)}, f32[384]{0:T(512)}, u32[]{:S(2)}) copy-start(f32[384]{0:T(512)} %param.34) | copy-start | bytes 4612
  85.8 7.4 %copy-start.66 = (f32[2048]{0:T(1024)}, f32[2048]{0:T(1024)S(1)}, u32[]{:S(2)}) copy-start(f32[2048]{0:T(1024)S(1)} %fusion.72) | copy-start | bytes 24580
  116.1 9.8 %copy-start.42 = (bf16[8,6,128,64]{2,3,1,0:T(8,128)(2,1)S(1)}, bf16[8,6,128,64]{2,3,1,0:T(8,128)(2,1)}, u32[]{:S(2)}) copy-start(bf16[8,6,128,64]{2,3,1,0:T(8,128)(2,1)} %copy-done.41) | copy-start | bytes 2359300
  125.9 5.6 copy-start.79
  125.9 5.6 copy-start.82
  125.9 5.6 copy-start.93
  125.9 5.6 copy-start.96
  125.9 5.6 copy-start.100
  125.9 5.6 copy-start.103
  125.9 5.6 copy-start.114
  131.5 8.6 %copy-start.15 = (f32[8,6,128,64]{2,3,1,0:T(8,128)}, f32[8,6,128,64]{2,3,1,0:T(8,128)S(1)}, u32[]{:S(2)}) copy-start(f32[8,6,128,64]{2,3,1,0:T(8,128)S(1)} %fusion.41) | copy-start | bytes 4718596
  135.1 5.0 copy-start.26
  135.1 5.0 copy-start.34
  140.1 5.3 copy-start.31
  148.0 4.7 copy-start.16
  148.0 4.7 copy-start.22
  148.0 4.7 copy-start.32
  148.0 4.7 copy-start.83
  148.0 4.7 copy-start.94
  179.5 6.5 copy-start.2
  179.5 6.5 copy-start.57
  179.5 6.5 copy-start.59
  179.5 6.5 copy-start.61
  201.3 310.0 %all-gather.3.cloned.1.call-start = ((), (), s32[]{:S(2)}) async-start(), calls=%async_computation | async-start | bytes 31457280 | tf_op jit(solution)/shard_map/all_gather | solution.py:161
  208.1 467.8 %all-reduce.24.cloned.1.call-start = ((), (), s32[]{:S(2)}) async-start(), calls=%async_computation.1 | async-start | bytes 8650752 | tf_op jit(solution)/shard_map/psum | solution.py:305
  208.1 5.4 copy-start.5
  208.1 5.4 copy-start.13
  208.2 8.2 %copy-start.17 = (bf16[2048,768]{1,0:T(8,128)(2,1)S(1)}, bf16[2048,768]{1,0:T(8,128)(2,1)}, u32[]{:S(2)}) copy-start(bf16[2048,768]{1,0:T(8,128)(2,1)} %param.19) | copy-start | bytes 9437188
  367.8 4.9 copy-start.36
  367.8 4.9 copy-start.65
  367.8 4.9 copy-start.76
  368.7 4.1 copy-start.8
  372.7 9.0 %copy-start.122 = (f32[384]{0:T(512)S(1)}, f32[384]{0:T(512)}, u32[]{:S(2)}) copy-start(f32[384]{0:T(512)} %get-tuple-element.21) | copy-start | bytes 4612
  511.3 12.9 %copy-start.77 = (f32[2048]{0:T(1024)S(1)}, f32[2048]{0:T(1024)}, u32[]{:S(2)}) copy-start(f32[2048]{0:T(1024)} %get-tuple-element.118) | copy-start | bytes 24580
  675.9 4.4 copy-start.37
  (68 other events, 150.2 us)
Sparse Core Ops, SparseCore 0:
  201.4 153.2 all-reduce.25
  356.3 154.9 all-gather.2
  516.4 159.4 all-reduce.23
